TPU v7x, 512 devices: a whole 4x4x16 slice. The times are simulated.
512 devices in a mesh: wide: 64 (over x, z), narrow: 8 (over y, core).
Axes of the slice: x: 4, y: 4, z: 16, core: 2. Of those that a mesh axis runs over, the one named last changes fastest.
Arguments:
- amplitudes: bfloat16 [2048, 8192], P(('wide', 'narrow')), may hold values from -6 to 6
- amp_mask: int32 [32, 128], replicated, may hold values from 0 to 1, as said below
- integrals: bfloat16 [2048, 32768], P('narrow', 'wide'), may hold values from -0.59765625 to 0.59765625
- int_mask: int32 [32, 512], replicated, may hold values from 0 to 1, as said below
- owner: int32 [512], replicated, may hold values from 0 to 511, each once
- occ_energy: float32 [8192], P('narrow'), may hold values from -3 to -0.5
- vir_energy: float32 [32768], replicated, may hold values from 1 to 8
Outputs:
- update: bfloat16 [8192, 32768], P('narrow', 'wide')
Inputs may be any that keep to these rules, and one draw needn't show every extreme that they name: `amp_mask`: 1 marks a pair of tiles within the screening distance, 0 one outside it. `int_mask`: 1 marks a pair of tiles within the screening distance, 0 one outside it. A permutation of the 512 tiles; columns 64 * s to 64 * s + 63 of integrals and update belong to tile owner[s].
All inputs are finite; a program needn't handle non-finite values.
Results may differ from a plain program's by a relative error of at most 0.001.
Values may be sent and summed in bfloat16 or wider, within the bound.
No kernel may reach another device: no remote copies, remote signals or barrier semaphores. Data moves between devices by JAX's collectives and lax.ppermute only.
A program may use at most 64 MiB of HBM per device.

v0:
```python
import jax
import jax.numpy as jnp
from jax import lax
from jax.sharding import PartitionSpec as P

TILE = 64


def contract_rows(summed, rows_in, int_part):
    return summed + lax.dot_general(
        rows_in, int_part, (((0,), (0,)), ((), ())), preferred_element_type=jnp.float32
    )


def contract_all(amp_full, int_full, starting):
    k_total = amp_full.shape[0]
    block_rows = min(512, k_total)
    summed = starting
    for first_row in range(0, k_total, block_rows):
        summed = contract_rows(
            summed,
            amp_full[first_row : first_row + block_rows],
            int_full[first_row : first_row + block_rows],
        )
    return summed


def shards(amplitudes, amp_mask, integrals, int_mask, owner, occ_energy, vir_energy):
    tile_width = TILE
    wide_count = lax.axis_size("wide")
    narrow_count = lax.axis_size("narrow")
    wide_index = lax.axis_index("wide")
    narrow_index = lax.axis_index("narrow")
    src_rows = amplitudes.shape[0]
    occ_all = amplitudes.shape[1]
    occ_here = occ_energy.shape[0]
    vir_here = integrals.shape[1]
    k_total = src_rows * wide_count * narrow_count
    first_src = (wide_index * narrow_count + narrow_index) * src_rows
    src_tiles = (first_src + jnp.arange(src_rows, dtype=jnp.int32)) // tile_width
    src_mask = jnp.take(amp_mask, src_tiles, axis=0)
    src_wide = jnp.broadcast_to(
        src_mask[:, :, None], (src_rows, occ_all // tile_width, tile_width)
    ).reshape(src_rows, occ_all)
    masked = jnp.where(src_wide == 1, amplitudes, jnp.zeros((), amplitudes.dtype))
    vir_tiles_here = vir_here // tile_width
    slot_ids = wide_index * vir_tiles_here + jnp.arange(vir_tiles_here, dtype=jnp.int32)
    tile_ids = jnp.take(owner, slot_ids)
    vir_mask = jnp.take(int_mask, tile_ids, axis=1)
    int_rows = integrals.shape[0]
    row_tiles = int_rows // tile_width
    local_mask = lax.dynamic_slice_in_dim(vir_mask, narrow_index * row_tiles, row_tiles, 0)
    local_wide = jnp.broadcast_to(
        local_mask[:, None, :, None], (row_tiles, tile_width, vir_tiles_here, tile_width)
    ).reshape(int_rows, vir_here)
    int_masked = jnp.where(local_wide == 1, integrals, jnp.zeros((), integrals.dtype))
    int_full = lax.all_gather(int_masked, "narrow", axis=0, tiled=True)
    starting = jnp.zeros((occ_here, vir_here), jnp.float32)
    wide_rows = lax.all_gather(masked, "wide", axis=0, tiled=True)
    blocked = lax.all_to_all(wide_rows, "narrow", split_axis=1, concat_axis=0, tiled=True)
    ordered = (
        blocked.reshape(narrow_count, wide_count, src_rows, occ_here)
        .transpose(1, 0, 2, 3)
        .reshape(k_total, occ_here)
    )
    ladder = contract_all(ordered, int_full, starting)
    vir_energy_here = jnp.take(vir_energy.reshape(-1, tile_width), tile_ids, axis=0).reshape(
        vir_here
    )
    denominator = vir_energy_here[None, :] - occ_energy[:, None]
    return (ladder / denominator).astype(jnp.bfloat16)


def solution(mesh):
    return jax.shard_map(
        shards,
        mesh=mesh,
        in_specs=(
            P(("wide", "narrow"), None),
            P(),
            P("narrow", "wide"),
            P(),
            P(),
            P("narrow"),
            P(),
        ),
        out_specs=P("narrow", "wide"),
        check_vma=False,
    )
```

profile of v0, /device:TPU:1, one launch (start us, length us, event | category | flops | bytes accessed | tf_op | source)
XLA Modules:
  0.0 269.0 jit_solution(17122527610451207436)
XLA Ops:
  7.4 0.0 copy-start
  7.4 0.0 all-gather.6.cloned.1.call-start
  7.4 0.7 copy-done
  8.1 0.6 gather_fusion
  8.6 0.1 select_compare_fusion
  8.7 0.1 broadcast_in_dim.55
  8.9 0.2 eq.22
  9.0 1.5 select_bitcast_fusion
  10.5 0.0 all-gather.6.cloned.1.call-update
  10.6 1.0 copy.21
  11.6 1.3 gather_fusion.1
  12.9 0.6 gather_fusion.2
  13.5 139.6 %all-gather.6.cloned.1.call-done = bf16[64,4,8192]{2,1,0:T(4,128)(2,1)} async-done(((bf16[1,4,8192]{2,1,0:T(4,128)(2,1)}), bf16[64,4,8192]{2,1,0:T(4,128)(2,1)}) %all-gather.6.cloned.1.call-update) | async-done | bytes 4194320 | tf_op jit(solution)/shard_map/all_gather | solution.py:59
  153.1 7.8 %all_to_all.12 = bf16[256,8,1024]{2,1,0:T(8,128)(2,1)} reshape(bf16[64,4,8192]{2,1,0:T(4,128)(2,1)} %all-gather.6.cloned.1.call-done) | data formatting | bytes 8388608 | tf_op jit(solution)/shard_map/all_to_all | solution.py:60
  160.9 6.5 %copy.18 = bf16[256,8,1024]{2,0,1:T(8,128)(2,1)} copy(bf16[256,8,1024]{2,1,0:T(8,128)(2,1)} %all_to_all.12) | data formatting | bytes 8388608 | tf_op jit(solution)/shard_map/all_to_all | solution.py:60
  167.3 14.7 %all-to-all-start = ((bf16[256,8,1024]{2,0,1:T(8,128)(2,1)}), bf16[256,8,1024]{2,0,1:T(8,128)(2,1)}, u32[]{:S(2)}, u32[]{:S(2)}) async-start(bf16[256,8,1024]{2,0,1:T(8,128)(2,1)} %copy.18), calls=%async_computation | async-start | bytes 8388608 | tf_op jit(solution)/shard_map/all_to_all | solution.py:60
  182.1 0.0 all-gather.4.cloned.1.call-start
  182.1 0.1 broadcast_select_fusion.1
  182.1 0.1 fusion.7
  182.2 0.1 copy.22
  182.3 0.1 broadcast_in_dim.59
  182.5 0.4 eq.25
  182.8 0.0 copy-done.3
  182.9 0.7 broadcast_select_fusion
  183.6 0.0 all-gather.4.cloned.1.call-update
  183.6 0.1 reshape.172
  183.7 0.6 gather_fusion.3
  184.3 0.1 broadcast_select_fusion.2
  184.4 0.1 select_n.135
  184.5 54.8 %all-to-all-done = bf16[256,8,1024]{2,0,1:T(8,128)(2,1)} async-done(((bf16[256,8,1024]{2,0,1:T(8,128)(2,1)}), bf16[256,8,1024]{2,0,1:T(8,128)(2,1)}, u32[]{:S(2)}, u32[]{:S(2)}) %all-to-all-start) | async-done | bytes 4194336 | tf_op jit(solution)/shard_map/all_to_all | solution.py:60
  239.3 4.5 %copy.19 = bf16[256,8,1024]{2,1,0:T(8,128)(2,1)S(1)} copy(bf16[256,8,1024]{2,0,1:T(8,128)(2,1)} %all-to-all-done) | data formatting | bytes 8388608 | tf_op jit(solution)/shard_map/all_to_all | solution.py:60
  243.8 1.8 fusion.11
  245.6 0.9 copy.25
  246.5 1.1 slice.46
  247.6 0.9 copy.24
  248.5 0.3 slice.43
  248.8 2.1 copy.23
  250.9 0.3 slice.40
  251.2 3.1 %copy.20 = bf16[16,8,4,1024]{3,2,1,0:T(4,128)(2,1)} copy(bf16[16,8,4,1024]{3,1,2,0:T(8,128)(2,1)} %get-tuple-element.8) | data formatting | bytes 2097152 | tf_op jit(solution)/shard_map/slice | solution.py:22
  254.3 1.3 slice.37
  255.6 0.0 all-gather.4.cloned.1.call-done
  255.7 1.9 fusion.1
  257.6 0.0 copy-done.1
  257.6 0.8 fusion.3
  258.4 0.0 copy-start.5
  258.4 0.7 fusion.5
  259.1 0.5 copy-done.2
  259.6 1.9 divide_convert_fusion
  (14 shorter events, 0.1 us)
Async XLA Ops:
  7.4 0.7 copy-start
  7.4 145.7 %all-gather.6.cloned.1.call-start = ((), (), s32[]{:S(2)}) async-start(), calls=%async_computation.2 | async-start | bytes 4259840 | tf_op jit(solution)/shard_map/all_gather | solution.py:59
  167.3 15.5 %copy-start.3 = (bf16[256,512]{1,0:T(8,128)(2,1)S(1)}, bf16[256,512]{1,0:T(8,128)(2,1)}, u32[]{:S(2)}) copy-start(bf16[256,512]{1,0:T(8,128)(2,1)} %param.9) | copy-start | bytes 786436
  167.3 16.3 %copy-start.4 = (f32[32768]{0:T(1024)S(1)}, f32[32768]{0:T(1024)}, u32[]{:S(2)}) copy-start(f32[32768]{0:T(1024)} %param.13) | copy-start | bytes 393220
  167.3 72.0 %all-to-all-start = ((bf16[256,8,1024]{2,0,1:T(8,128)(2,1)}), bf16[256,8,1024]{2,0,1:T(8,128)(2,1)}, u32[]{:S(2)}, u32[]{:S(2)}) async-start(bf16[256,8,1024]{2,0,1:T(8,128)(2,1)} %copy.18), calls=%async_computation | async-start | bytes 8388608 | tf_op jit(solution)/shard_map/all_to_all | solution.py:60
  182.1 73.6 %all-gather.4.cloned.1.call-start = ((), (), s32[]{:S(2)}) async-start(), calls=%async_computation.1 | async-start | bytes 2359296 | tf_op jit(solution)/shard_map/all_gather | solution.py:57
  255.7 1.9 copy-start.1
  258.4 1.2 copy-start.2
  258.4 1.2 copy-start.5
Sparse Core Ops, SparseCore 0:
  11.1 141.9 all-gather.5
Sparse Core Ops, SparseCore 1:
  184.7 34.4 all-gather.3
where the time goes:
time: 270 us; the launch traced here: 269 us
  waiting for transfers between devices  194 us (72%)
  local copies, waits for them, and re-layouts  36.7 us (14%)
  between operations  15 us (6%)
  starting transfers between devices  14.7 us (5%)
  matrix products  5.37 us (2%)
    all_gather x1, waiting for transfers between devices, shards(): wide_rows = lax.all_gather(masked, 'wide', axis=0, tiled=True)  140 us
    all_to_all x1, waiting for transfers between devices, shards(): lax.all_to_all(wide_rows, 'narrow', split_axis=1, concat_axis=0, tiled=True)  54.8 us
    all_to_all x3, local copies, waits for them, and re-layouts, shards(): lax.all_to_all(wide_rows, 'narrow', split_axis=1, concat_axis=0, tiled=True)  18.7 us
    all_to_all x1, starting transfers between devices, shards(): lax.all_to_all(wide_rows, 'narrow', split_axis=1, concat_axis=0, tiled=True)  14.7 us
    slice x9, local copies, waits for them, and re-layouts, contract_all(): amp_full[first_row:first_row + block_rows]  11.8 us
  transfers between devices with their start and end apart: 3, of which 2 were waited for; matrix products, arithmetic and copies ran while one was open for 8% of the time, Pallas kernels for 0%

commit v1 on v0

--- a/solution.py
+++ b/solution.py
@@ -56,7 +56,8 @@
     int_masked = jnp.where(local_wide == 1, integrals, jnp.zeros((), integrals.dtype))
     int_full = lax.all_gather(int_masked, "narrow", axis=0, tiled=True)
     starting = jnp.zeros((occ_here, vir_here), jnp.float32)
-    wide_rows = lax.all_gather(masked, "wide", axis=0, tiled=True)
+    outgoing = jnp.stack([masked] * lax.axis_size("wide"))
+    wide_rows = jnp.concatenate(lax.all_to_all(outgoing, "wide", 0, 0), axis=0)
     blocked = lax.all_to_all(wide_rows, "narrow", split_axis=1, concat_axis=0, tiled=True)
     ordered = (
         blocked.reshape(narrow_count, wide_count, src_rows, occ_here)

time: 270 us -> 331 us (1.23)
  waiting for transfers between devices: 194 us -> 237 us
  starting transfers between devices: 14.7 us -> 29.4 us
  local copies, waits for them, and re-layouts: 36.7 us -> 42.4 us
    all_to_all x0 -> x1, waiting for transfers between devices: none -> 182 us  [shards(): wide_rows = jnp.concatenate(lax.all_to_all(outgoing, 'wide', 0, 0), axis=0)]
    all_gather x1 -> x0, waiting for transfers between devices: 140 us -> none  [shards(): wide_rows = lax.all_gather(masked, 'wide', axis=0, tiled=True)]
    all_to_all x0 -> x1, starting transfers between devices: none -> 19.5 us  [shards(): wide_rows = jnp.concatenate(lax.all_to_all(outgoing, 'wide', 0, 0), axis=0)]
    all_to_all x1, starting transfers between devices: 14.7 us -> 9.92 us  [shards(): lax.all_to_all(wide_rows, 'narrow', split_axis=1, concat_axis=0, tiled=True)]
    another operation x0 -> x1, local copies, waits for them, and re-layouts: none -> 3.99 us  [shards(): outgoing = jnp.stack([masked] * lax.axis_size('wide'))]
  transfers between devices with their start and end apart: 3 -> 3, of which waited for: 2 -> 2; matrix products, arithmetic and copies ran while one was open for 8% -> 7% of each run, Pallas kernels for 0% -> 0%
where the time goes in v1:
time: 331 us; the launch traced here: 330 us
  waiting for transfers between devices  237 us (72%)
  local copies, waits for them, and re-layouts  42.4 us (13%)
  starting transfers between devices  29.4 us (9%)
  between operations  13.6 us (4%)
  matrix products  5.37 us (2%)
    all_to_all x1, waiting for transfers between devices, shards(): wide_rows = jnp.concatenate(lax.all_to_all(outgoing, 'wide', 0, 0), axis=0)  182 us
    all_to_all x1, waiting for transfers between devices, shards(): lax.all_to_all(wide_rows, 'narrow', split_axis=1, concat_axis=0, tiled=True)  54.8 us
    all_to_all x1, starting transfers between devices, shards(): wide_rows = jnp.concatenate(lax.all_to_all(outgoing, 'wide', 0, 0), axis=0)  19.5 us
    all_to_all x3, local copies, waits for them, and re-layouts, shards(): lax.all_to_all(wide_rows, 'narrow', split_axis=1, concat_axis=0, tiled=True)  18.8 us
    slice x9, local copies, waits for them, and re-layouts, contract_all(): amp_full[first_row:first_row + block_rows]  15 us
    all_to_all x1, starting transfers between devices, shards(): lax.all_to_all(wide_rows, 'narrow', split_axis=1, concat_axis=0, tiled=True)  9.92 us
  transfers between devices with their start and end apart: 3, of which 2 were waited for; matrix products, arithmetic and copies ran while one was open for 7% of the time, Pallas kernels for 0%

profile of v1, /device:TPU:1, one launch (start us, length us, event | category | flops | bytes accessed | tf_op | source)
XLA Modules:
  0.0 329.7 jit_solution(7224053824859371581)
XLA Ops:
  6.5 0.0 copy-start
  6.6 0.7 copy-done
  7.3 0.6 gather_fusion
  7.8 0.1 select_compare_fusion
  7.9 0.1 broadcast_in_dim.55
  8.0 0.2 eq.22
  8.2 0.9 broadcast_select_fusion.1
  9.1 4.0 %stack.2 = bf16[64,4,8192]{2,1,0:T(4,128)(2,1)} broadcast(bf16[4,8192]{1,0:T(4,128)(2,1)S(1)} %broadcast_select_fusion.1), dimensions={1,2} | broadcast | bytes 4259840 | tf_op jit(solution)/shard_map/stack | solution.py:59
  13.1 19.5 %all-to-all-start = ((bf16[64,4,8192]{2,1,0:T(4,128)(2,1)}), bf16[64,4,8192]{2,1,0:T(4,128)(2,1)}, u32[]{:S(2)}, u32[]{:S(2)}) async-start(bf16[64,4,8192]{2,1,0:T(4,128)(2,1)} %stack.2), calls=%async_computation | async-start | bytes 8388608 | tf_op jit(solution)/shard_map/all_to_all | solution.py:60
  32.6 0.1 copy.28
  32.7 0.0 copy-done.1
  32.8 0.6 gather_fusion.1
  33.4 0.6 gather_fusion.2
  34.0 182.1 %all-to-all-done = bf16[64,4,8192]{2,1,0:T(4,128)(2,1)} async-done(((bf16[64,4,8192]{2,1,0:T(4,128)(2,1)}), bf16[64,4,8192]{2,1,0:T(4,128)(2,1)}, u32[]{:S(2)}, u32[]{:S(2)}) %all-to-all-start) | async-done | bytes 4194336 | tf_op jit(solution)/shard_map/all_to_all | solution.py:60
  216.1 7.8 %all_to_all.16 = bf16[256,8,1024]{2,1,0:T(8,128)(2,1)} reshape(bf16[64,4,8192]{2,1,0:T(4,128)(2,1)} %all-to-all-done) | data formatting | bytes 8388608 | tf_op jit(solution)/shard_map/all_to_all | solution.py:61
  223.9 6.5 %copy.25 = bf16[256,8,1024]{2,0,1:T(8,128)(2,1)} copy(bf16[256,8,1024]{2,1,0:T(8,128)(2,1)} %all_to_all.16) | data formatting | bytes 8388608 | tf_op jit(solution)/shard_map/all_to_all | solution.py:61
  230.3 9.9 %all-to-all-start.1 = ((bf16[256,8,1024]{2,0,1:T(8,128)(2,1)}), bf16[256,8,1024]{2,0,1:T(8,128)(2,1)}, u32[]{:S(2)}, u32[]{:S(2)}) async-start(bf16[256,8,1024]{2,0,1:T(8,128)(2,1)} %copy.25), calls=%async_computation.1 | async-start | bytes 8388608 | tf_op jit(solution)/shard_map/all_to_all | solution.py:61
  240.3 0.0 all-gather.2.cloned.1.call-start
  240.3 0.1 broadcast_select_fusion.2
  240.3 0.1 fusion.7
  240.4 0.1 copy.29
  240.5 0.1 broadcast_in_dim.59
  240.6 0.4 eq.25
  241.0 0.7 broadcast_select_fusion
  241.8 0.0 all-gather.2.cloned.1.call-update
  241.8 0.1 reshape.176
  241.9 0.6 gather_fusion.3
  242.5 0.1 broadcast_select_fusion.3
  242.6 0.1 select_n.135
  242.6 54.8 %all-to-all-done.1 = bf16[256,8,1024]{2,0,1:T(8,128)(2,1)} async-done(((bf16[256,8,1024]{2,0,1:T(8,128)(2,1)}), bf16[256,8,1024]{2,0,1:T(8,128)(2,1)}, u32[]{:S(2)}, u32[]{:S(2)}) %all-to-all-start.1) | async-done | bytes 4194336 | tf_op jit(solution)/shard_map/all_to_all | solution.py:61
  297.5 4.5 %copy.26 = bf16[256,8,1024]{2,1,0:T(8,128)(2,1)S(1)} copy(bf16[256,8,1024]{2,0,1:T(8,128)(2,1)} %all-to-all-done.1) | data formatting | bytes 8388608 | tf_op jit(solution)/shard_map/all_to_all | solution.py:61
  302.0 1.8 fusion.11
  303.7 0.9 copy.31
  304.6 0.3 slice.43
  304.9 2.1 copy.27
  307.0 0.3 slice.37
  307.3 3.1 copy.30
  310.4 1.3 slice.40
  311.7 3.1 copy.32
  314.8 2.1 slice.46
  317.0 1.9 fusion.1
  318.9 0.7 fusion.5
  319.7 0.0 copy-start.3
  319.7 0.0 copy-start.7
  319.7 0.7 fusion.3
  320.4 0.5 copy-done.3
  320.9 0.0 copy-done.7
  320.9 1.9 divide_convert_fusion
  (18 shorter events, 0.1 us)
Async XLA Ops:
  6.5 0.7 copy-start
  13.1 19.5 %copy-start.6 = (s32[32,512]{1,0:T(8,128)S(1)}, s32[32,512]{1,0:T(8,128)}, u32[]{:S(2)}) copy-start(s32[32,512]{1,0:T(8,128)} %param.10) | copy-start | bytes 196612
  13.1 19.7 %copy-start.1 = (s32[512]{0:T(512)S(1)}, s32[512]{0:T(512)}, u32[]{:S(2)}) copy-start(s32[512]{0:T(512)} %param.11) | copy-start | bytes 6148
  13.1 203.0 %all-to-all-start = ((bf16[64,4,8192]{2,1,0:T(4,128)(2,1)}), bf16[64,4,8192]{2,1,0:T(4,128)(2,1)}, u32[]{:S(2)}, u32[]{:S(2)}) async-start(bf16[64,4,8192]{2,1,0:T(4,128)(2,1)} %stack.2), calls=%async_computation | async-start | bytes 8388608 | tf_op jit(solution)/shard_map/all_to_all | solution.py:60
  230.3 10.7 %copy-start.4 = (bf16[256,512]{1,0:T(8,128)(2,1)S(1)}, bf16[256,512]{1,0:T(8,128)(2,1)}, u32[]{:S(2)}) copy-start(bf16[256,512]{1,0:T(8,128)(2,1)} %param.9) | copy-start | bytes 786436
  230.3 11.5 %copy-start.5 = (f32[32768]{0:T(1024)S(1)}, f32[32768]{0:T(1024)}, u32[]{:S(2)}) copy-start(f32[32768]{0:T(1024)} %param.13) | copy-start | bytes 393220
  230.3 67.1 %all-to-all-start.1 = ((bf16[256,8,1024]{2,0,1:T(8,128)(2,1)}), bf16[256,8,1024]{2,0,1:T(8,128)(2,1)}, u32[]{:S(2)}, u32[]{:S(2)}) async-start(bf16[256,8,1024]{2,0,1:T(8,128)(2,1)} %copy.25), calls=%async_computation.1 | async-start | bytes 8388608 | tf_op jit(solution)/shard_map/all_to_all | solution.py:61
  240.3 76.7 %all-gather.2.cloned.1.call-start = ((), (), s32[]{:S(2)}) async-start(), calls=%async_computation.2 | async-start | bytes 2359296 | tf_op jit(solution)/shard_map/all_gather | solution.py:57
  317.0 1.9 copy-start.2
  319.7 1.2 copy-start.3
  319.7 1.2 copy-start.7
Sparse Core Ops, SparseCore 0:
  243.2 33.0 all-gather.1
